TPU v7x, 32 devices: a whole 2x2x4 slice. The times are simulated.
32 devices in a mesh: dp: 32 (over z, y, x, core).
Axes of the slice: x: 2, y: 2, z: 4, core: 2. Of those that a mesh axis runs over, the one named last changes fastest.
Arguments:
- tokens: bfloat16 [24576, 1024], P('dp'), may hold values from -6 to 6
- seg_ids: int32 [96, 256], P('dp'), may hold values from 0 to 7, never falling along the last dimension, each value on 1 to 128 neighbouring positions
- w_qkv: bfloat16 [1024, 3072], P('dp'), may hold values from -0.1875 to 0.1875
- w_attn_out: bfloat16 [1024, 1024], P('dp'), may hold values from -1 to 1
- w_in: bfloat16 [1024, 5248], P('dp'), may hold values from -0.1875 to 0.1875
- w_down: bfloat16 [2624, 1024], P(None, 'dp'), may hold values from -0.125 to 0.125
- gain_attn: bfloat16 [1024], P('dp'), may hold values from 0.099609375 to 1.8984375
- gain_mlp: bfloat16 [1024], P('dp'), may hold values from 0.099609375 to 1.8984375
- cotangent: bfloat16 [24576, 1024], P('dp'), may hold values from -6 to 6
Outputs:
- out: bfloat16 [24576, 1024], P('dp')
- tokens_grad: float32 [24576, 1024], P('dp')
- grad_qkv: float32 [1024, 3072], P('dp')
- grad_attn_out: float32 [1024, 1024], P('dp')
- grad_in: float32 [1024, 5248], P('dp')
- grad_down: float32 [2624, 1024], P(None, 'dp')
- grad_gain_attn: float32 [1024], P('dp')
- grad_gain_mlp: float32 [1024], P('dp')
Inputs may be any that keep to these rules, and one draw needn't show every extreme that they name: `seg_ids`: in each micro-batch the numbers never fall along the 256 slots and all 8 numbers occur; each run of equal numbers is one sequence of 1 to 128 tokens, and some run in the draw is exactly 128 long.
All inputs are finite; a program needn't handle non-finite values.
Results may differ from a plain program's by a relative error of at most 0.012.
The roundings to bfloat16 on the way count: a program that leaves them out, or rounds other values in their place, can miss the bound.
Values may be sent and summed in bfloat16 or wider, within the bound.
No kernel may reach another device: no remote copies, remote signals or barrier semaphores. Data moves between devices by JAX's collectives and lax.ppermute only.
A program may use at most 256 MiB of HBM per device.

v0:
```python
import jax
import jax.numpy as jnp
from jax import lax
from jax.sharding import PartitionSpec as P

HEADS = 16
HEAD_DIM = 64
EPSILON = 1e-05
THETA = 160000.0
NEG_BIG = -1e30
ROOT_HALF = 0.7071067811865476
INV_ROOT_TWO_PI = 0.3989422804014327


def positions(seg_row):
    column = lax.broadcasted_iota(jnp.int32, seg_row.shape, seg_row.ndim - 1)
    before = jnp.concatenate(
        [jnp.full(seg_row.shape[:-1] + (1,), -1, jnp.int32), seg_row[..., :-1]], axis=-1
    )
    starts = lax.cummax(jnp.where(seg_row != before, column, 0), axis=seg_row.ndim - 1)
    return column - starts


def rotary_tables(offsets):
    halves = HEAD_DIM // 2
    frequency = jnp.power(
        jnp.float32(THETA), -(jnp.arange(halves, dtype=jnp.float32) * 2.0 / HEAD_DIM)
    )
    angles = offsets.astype(jnp.float32)[:, None] * frequency[None, :]
    angles = jnp.concatenate([angles, angles], axis=-1)
    return (jnp.cos(angles)[:, None, :], jnp.sin(angles)[:, None, :])


def rotate(field):
    halves = field.shape[-1] // 2
    return jnp.concatenate([-field[..., halves:], field[..., :halves]], axis=-1)


def rotate_back(field):
    halves = field.shape[-1] // 2
    return jnp.concatenate([field[..., halves:], -field[..., :halves]], axis=-1)


def gelu_exact(field):
    return 0.5 * field * (1.0 + lax.erf(field * ROOT_HALF))


def gelu_slope(field):
    return (
        0.5 * (1.0 + lax.erf(field * ROOT_HALF))
        + field * jnp.exp(-0.5 * field * field) * INV_ROOT_TWO_PI
    )


def norm_forward(field, gain_row):
    center = field - jnp.mean(field, axis=-1, keepdims=True)
    inv_scale = lax.rsqrt(jnp.mean(center * center, axis=-1, keepdims=True) + EPSILON)
    unit_rows = center * inv_scale
    return (unit_rows * gain_row, unit_rows, inv_scale)


def norm_backward(gradient, unit_rows, inv_scale, gain_row):
    scaled = gradient * gain_row
    inner = (
        scaled
        - jnp.mean(scaled, axis=-1, keepdims=True)
        - unit_rows * jnp.mean(scaled * unit_rows, axis=-1, keepdims=True)
    )
    return (inv_scale * inner, jnp.sum(gradient * unit_rows, axis=0))


def score_block(queries, keys_rot, seg_row):
    scores = jnp.einsum(
        "qhd,khd->hqk", queries, keys_rot, preferred_element_type=jnp.float32
    ) * HEAD_DIM ** (-0.5)
    same_seq = seg_row[:, None] == seg_row[None, :]
    return jnp.where(same_seq[None], scores, NEG_BIG)


def attend(queries, keys_rot, values, seg_row):
    scores = score_block(queries, keys_rot, seg_row)
    row_max = jnp.max(scores, axis=-1, keepdims=True)
    exponent = jnp.exp(scores - row_max)
    row_total = jnp.sum(exponent, axis=-1, keepdims=True)
    probability = (exponent / row_total).astype(jnp.bfloat16)
    attended = jnp.einsum("hqk,khd->qhd", probability, values, preferred_element_type=jnp.float32)
    return (attended.astype(jnp.bfloat16), row_max, row_total)


def attend_backward(queries, keys_rot, values, seg_row, row_max, row_total, grad_att):
    scores = score_block(queries, keys_rot, seg_row)
    probability = jnp.exp(scores - row_max) / row_total
    grad_prob = jnp.einsum("qhd,khd->hqk", grad_att, values, preferred_element_type=jnp.float32)
    grad_values = jnp.einsum(
        "hqk,qhd->khd",
        probability.astype(jnp.bfloat16),
        grad_att,
        preferred_element_type=jnp.float32,
    )
    grad_scores = probability * (
        grad_prob - jnp.sum(grad_prob * probability, axis=-1, keepdims=True)
    )
    grad_scores = grad_scores.astype(jnp.bfloat16)
    grad_queries = jnp.einsum(
        "hqk,khd->qhd", grad_scores, keys_rot, preferred_element_type=jnp.float32
    ) * HEAD_DIM ** (-0.5)
    grad_keys = jnp.einsum(
        "hqk,qhd->khd", grad_scores, queries, preferred_element_type=jnp.float32
    ) * HEAD_DIM ** (-0.5)
    return (grad_queries, grad_keys, grad_values)


def shards(tokens, seg_ids, w_qkv, w_attn_out, w_in, w_down, gain_attn, gain_mlp, cotangent):
    micro_count, block_rows = seg_ids.shape
    model_width = tokens.shape[1]
    hidden_units = w_down.shape[0]

    def weights_now():
        return (
            lax.all_gather(w_qkv, "dp", axis=0, tiled=True),
            lax.all_gather(w_attn_out, "dp", axis=0, tiled=True),
            lax.all_gather(w_in, "dp", axis=0, tiled=True),
            lax.all_gather(w_down, "dp", axis=1, tiled=True),
            lax.all_gather(gain_attn, "dp", axis=0, tiled=True),
            lax.all_gather(gain_mlp, "dp", axis=0, tiled=True),
        )

    stored = []
    outputs = []
    for micro_index in range(micro_count):
        wq_full, wo_full, wi_full, wd_full, ga_full, gm_full = weights_now()
        lower = micro_index * block_rows
        inputs = tokens[lower : lower + block_rows].astype(jnp.float32)
        seg_row = seg_ids[micro_index]
        cosine_table, sine_table = rotary_tables(positions(seg_row))
        normed_attn, unit_attn, inv_attn = norm_forward(inputs, ga_full.astype(jnp.float32))
        normed_attn = normed_attn.astype(jnp.bfloat16)
        projected = jnp.dot(normed_attn, wq_full, preferred_element_type=jnp.float32)
        queries = projected[:, :model_width].reshape(block_rows, HEADS, HEAD_DIM)
        keys_rot = projected[:, model_width : 2 * model_width].reshape(block_rows, HEADS, HEAD_DIM)
        values = (
            projected[:, 2 * model_width :]
            .reshape(block_rows, HEADS, HEAD_DIM)
            .astype(jnp.bfloat16)
        )
        queries = (queries * cosine_table + rotate(queries) * sine_table).astype(jnp.bfloat16)
        keys_rot = (keys_rot * cosine_table + rotate(keys_rot) * sine_table).astype(jnp.bfloat16)
        attended, row_max, row_total = attend(queries, keys_rot, values, seg_row)
        attended = attended.reshape(block_rows, model_width)
        resid = inputs + jnp.dot(attended, wo_full, preferred_element_type=jnp.float32)
        normed_mlp, unit_mlp, inv_mlp = norm_forward(resid, gm_full.astype(jnp.float32))
        normed_mlp = normed_mlp.astype(jnp.bfloat16)
        gate_up = jnp.dot(normed_mlp, wi_full, preferred_element_type=jnp.float32)
        gate = gate_up[:, :hidden_units]
        upward = gate_up[:, hidden_units:]
        activated = gelu_exact(gate)
        hidden = (activated * upward).astype(jnp.bfloat16)
        result = resid + jnp.dot(hidden, wd_full, preferred_element_type=jnp.float32)
        outputs.append(result.astype(jnp.bfloat16))
        stored.append(
            (
                seg_row,
                cosine_table,
                sine_table,
                unit_attn,
                inv_attn,
                normed_attn,
                queries,
                keys_rot,
                values,
                row_max,
                row_total,
                attended,
                unit_mlp,
                inv_mlp,
                normed_mlp,
                gate,
                upward,
                activated,
                hidden,
            )
        )
    summed = None
    input_grads = []
    for micro_index in reversed(range(micro_count)):
        wq_full, wo_full, wi_full, wd_full, ga_full, gm_full = weights_now()
        (
            seg_row,
            cosine_table,
            sine_table,
            unit_attn,
            inv_attn,
            normed_attn,
            queries,
            keys_rot,
            values,
            row_max,
            row_total,
            attended,
            unit_mlp,
            inv_mlp,
            normed_mlp,
            gate,
            upward,
            activated,
            hidden,
        ) = stored[micro_index]
        lower = micro_index * block_rows
        grad_out_b = cotangent[lower : lower + block_rows]
        grad_out = grad_out_b.astype(jnp.float32)
        grad_down = jnp.dot(hidden.T, grad_out_b, preferred_element_type=jnp.float32)
        grad_hidden = jnp.dot(grad_out_b, wd_full.T, preferred_element_type=jnp.float32)
        grad_gate_up = jnp.concatenate(
            [grad_hidden * upward * gelu_slope(gate), grad_hidden * activated], axis=-1
        )
        grad_gate_up = grad_gate_up.astype(jnp.bfloat16)
        grad_in = jnp.dot(normed_mlp.T, grad_gate_up, preferred_element_type=jnp.float32)
        grad_normed_mlp = jnp.dot(grad_gate_up, wi_full.T, preferred_element_type=jnp.float32)
        resid_part, grad_gain_mlp = norm_backward(
            grad_normed_mlp, unit_mlp, inv_mlp, gm_full.astype(jnp.float32)
        )
        grad_resid = grad_out + resid_part
        grad_resid_b = grad_resid.astype(jnp.bfloat16)
        grad_attn = jnp.dot(attended.T, grad_resid_b, preferred_element_type=jnp.float32)
        grad_att = jnp.dot(grad_resid_b, wo_full.T, preferred_element_type=jnp.float32).astype(
            jnp.bfloat16
        )
        grad_att = grad_att.reshape(block_rows, HEADS, HEAD_DIM)
        grad_q_rot, grad_k_rot, grad_values = attend_backward(
            queries, keys_rot, values, seg_row, row_max, row_total, grad_att
        )
        grad_queries = grad_q_rot * cosine_table + rotate_back(grad_q_rot * sine_table)
        grad_keys = grad_k_rot * cosine_table + rotate_back(grad_k_rot * sine_table)
        grad_projected = jnp.concatenate(
            [
                grad_queries.reshape(block_rows, model_width),
                grad_keys.reshape(block_rows, model_width),
                grad_values.reshape(block_rows, model_width),
            ],
            axis=-1,
        ).astype(jnp.bfloat16)
        grad_qkv = jnp.dot(normed_attn.T, grad_projected, preferred_element_type=jnp.float32)
        grad_normed_attn = jnp.dot(grad_projected, wq_full.T, preferred_element_type=jnp.float32)
        input_part, grad_gain_attn = norm_backward(
            grad_normed_attn, unit_attn, inv_attn, ga_full.astype(jnp.float32)
        )
        input_grads.append(grad_resid + input_part)
        grads_now = (grad_qkv, grad_attn, grad_in, grad_down, grad_gain_attn, grad_gain_mlp)
        if summed is None:
            summed = grads_now
        else:
            summed = tuple((earlier + latest for earlier, latest in zip(summed, grads_now)))
    summed = (
        lax.psum_scatter(summed[0], "dp", scatter_dimension=0, tiled=True),
        lax.psum_scatter(summed[1], "dp", scatter_dimension=0, tiled=True),
        lax.psum_scatter(summed[2], "dp", scatter_dimension=0, tiled=True),
        lax.psum_scatter(summed[3], "dp", scatter_dimension=1, tiled=True),
        lax.psum_scatter(summed[4], "dp", scatter_dimension=0, tiled=True),
        lax.psum_scatter(summed[5], "dp", scatter_dimension=0, tiled=True),
    )
    return (
        jnp.concatenate(outputs, axis=0),
        jnp.concatenate(input_grads[::-1], axis=0),
        summed[0],
        summed[1],
        summed[2],
        summed[3],
        summed[4],
        summed[5],
    )


def solution(mesh):
    return jax.shard_map(
        shards,
        mesh=mesh,
        in_specs=(
            P("dp", None),
            P("dp", None),
            P("dp", None),
            P("dp", None),
            P("dp", None),
            P(None, "dp"),
            P("dp"),
            P("dp"),
            P("dp", None),
        ),
        out_specs=(
            P("dp", None),
            P("dp", None),
            P("dp", None),
            P("dp", None),
            P("dp", None),
            P(None, "dp"),
            P("dp"),
            P("dp"),
        ),
        check_vma=False,
    )
```

profile of v0, /device:TPU:14, one launch (start us, length us, event | category | flops | bytes accessed | tf_op | source)
XLA Modules:
  0.0 1046.7 jit_solution(11209581067904707399)
XLA Ops:
  14.5 41.1 %all-reduce.5 = (bf16[1024]{0:T(1024)(128)(2,1)S(1)}, bf16[1024]{0:T(1024)(128)(2,1)S(1)}) all-reduce(bf16[1024]{0:T(1024)(128)(2,1)S(1)} %dynamic-update-slice, bf16[1024]{0:T(1024)(128)(2,1)S(1)} %dynamic-update-slice.1), channel_id=1, replica_groups=mesh['dp'=32] {'dp'}, use_global_device_ids=true, to_apply=%add | all-reduce | flops 2048 | bytes 8192
  62.3 18.4 %all-gather.5.cloned.1.call-done = bf16[1024,3072]{1,0:T(8,128)(2,1)} async-done(((bf16[32,3072]{1,0:T(8,128)(2,1)}), bf16[1024,3072]{1,0:T(8,128)(2,1)}) %all-gather.5.cloned.1.call-update) | async-done | bytes 6291472 | tf_op jit(solution)/shard_map/all_gather | solution.py:120
  80.7 4.8 fusion.171
  102.0 4.7 fusion.165
  120.8 4.7 fusion.187
  128.4 9.3 all-gather.7.cloned.1.call-done
  154.1 4.7 fusion.191
  164.9 62.8 %all-gather.9.cloned.1.call-done = bf16[1024,5248]{1,0:T(8,128)(2,1)} async-done(((bf16[32,5248]{1,0:T(8,128)(2,1)}), bf16[1024,5248]{1,0:T(8,128)(2,1)}) %all-gather.9.cloned.1.call-update) | async-done | bytes 10747920 | tf_op jit(solution)/shard_map/all_gather | solution.py:122
  227.7 9.1 fusion.175
  236.8 5.1 fusion.174
  241.8 53.9 %all-gather.11.cloned.1.call-done = bf16[2624,1024]{0,1:T(8,128)(2,1)} async-done(((bf16[2624,32]{0,1:T(8,128)(2,1)}), bf16[2624,1024]{0,1:T(8,128)(2,1)}) %all-gather.11.cloned.1.call-update) | async-done | bytes 5373968 | tf_op jit(solution)/shard_map/all_gather | solution.py:123
  295.8 7.9 fusion.23
  303.7 7.1 fusion.17
  314.9 7.5 multiply_reduce_fusion.4
  326.9 9.5 fusion.11
  336.4 11.5 %multiply_add_fusion.1 = (f32[256,1024]{1,0:T(8,128)S(1)}, f32[256,1024]{1,0:T(8,128)}, f32[256]{0:T(256)S(1)}, f32[256]{0:T(256)S(1)}, f32[1024]{0:T(1024)}, /*index=5*/f32[256,1024]{1,0:T(8,128)}) fusion(f32[256,1024]{1,0:T(8,128)} %get-tuple-element.139, f32[256,1024]{1,0:T(8,128)S(1)} %copy-done.13, f32[256]{0:T(256)S(1)} %broadcast_multiply_fusion.21, ...), kind=kOutput, calls=%fused_computation.187 | convolution fusion | flops 2763651584 | bytes 22892544 | tf_op jit(solution)/shard_map/dot_general | solution.py:218
  359.3 6.8 fusion.113
  366.1 12.3 %add_add_fusion.2 = f32[2624,1024]{0,1:T(8,128)} fusion(f32[2624,1024]{0,1:T(8,128)S(1)} %fusion.109, f32[2624,1024]{0,1:T(8,128)} %fusion.113, bf16[768,1024]{1,0:T(8,128)(2,1)} %param.17, f32[256,5248]{1,0:T(8,128)} %copy-done.18), kind=kOutput, calls=%fused_computation.5 | convolution fusion | flops 1385136128 | bytes 38535168 | tf_op jit(solution)/shard_map/dot_general | solution.py:211
  414.4 6.6 fusion.104
  421.8 6.6 fusion.106
  429.2 13.8 %add_add_fusion.1 = f32[1024,3072]{1,0:T(8,128)} fusion(f32[1024,3072]{1,0:T(8,128)} %fusion.104, f32[1024,3072]{1,0:T(8,128)} %fusion.106, bf16[256,1024]{0,1:T(8,128)(2,1)S(1)} %bitcast.185, bf16[256,1024]{0,1:T(8,128)(2,1)S(1)} %bitcast.169, bf16[256,1024]{0,1:T(8,128)(2,1)S(1)} %bitcast.167, f32[1024]{0:T(1024)S(1)} %copy-done.71, ...), kind=kOutput, calls=%fused_computation.4 | convolution fusion | flops 1622933504 | bytes 39852032 | tf_op jit(solution)/shard_map/dot_general | solution.py:242
  444.3 11.0 %fusion.33 = f32[1024,5248]{1,0:T(8,128)} fusion(bf16[256,2624]{1,0:T(8,128)(2,1)} %copy-done.59, bf16[256,2624]{1,0:T(8,128)(2,1)} %copy-done.58, f32[256,1024]{1,0:T(8,128)S(1)} %copy-done.10, f32[256]{0:T(256)S(1)} %add_rsqrt_fusion, f32[256]{0:T(256)S(1)} %broadcast_multiply_fusion.27, f32[1024]{0:T(1024)S(1)} %convert_element_type.194), kind=kOutput, calls=%fused_computation.71 | convolution fusion | flops 2757885952 | bytes 25237504 | tf_op jit(solution)/shard_map/dot_general | solution.py:217
  455.4 9.2 fusion.35
  464.6 23.6 %add_add_fusion = f32[1024,5248]{1,0:T(8,128)} fusion(f32[1024,5248]{1,0:T(8,128)} %fusion.33, f32[1024,5248]{1,0:T(8,128)} %fusion.35, bf16[256,2624]{1,0:T(8,128)(2,1)S(1)} %copy-done.63, bf16[256,2624]{1,0:T(8,128)(2,1)S(1)} %copy-done.62, f32[256,1024]{1,0:T(8,128)S(1)} %copy-done.6, f32[1024]{0:T(1024)S(1)} %convert_element_type.194, ...), kind=kOutput, calls=%fused_computation.3 | convolution fusion | flops 2768633856 | bytes 68229120 | tf_op jit(solution)/shard_map/dot_general | solution.py:217
  488.2 5.2 fusion.107
  493.6 5.1 fusion.105
  502.4 40.0 %all-reduce.4 = (f32[1024]{0:T(1024)S(1)}, f32[1024]{0:T(1024)S(1)}) all-reduce(f32[1024]{0:T(1024)S(1)} %add_add_fusion.5, f32[1024]{0:T(1024)S(1)} %add_add_fusion.4), channel_id=6, replica_groups=mesh['dp'=32] {'dp'}, use_global_device_ids=true, to_apply=%region_46.47.clone | all-reduce | flops 2048 | bytes 16384
  543.7 5.1 fusion.40
  548.8 4.6 fusion.39
  561.3 80.5 %reduce-scatter.11.cloned.1.call-done = f32[2624,32]{0,1:T(8,128)} async-done(((f32[2624,1024]{0,1:T(8,128)}), f32[2624,32]{0,1:T(8,128)}) %reduce-scatter.11.cloned.1.call-update) | async-done | bytes 335888 | tf_op jit(solution)/shard_map/reduce_scatter | solution.py:257
  641.7 161.3 %reduce-scatter.5.cloned.1.call-done = f32[32,3072]{1,0:T(8,128)} async-done(((f32[1024,3072]{1,0:T(8,128)}), f32[32,3072]{1,0:T(8,128)}) %reduce-scatter.5.cloned.1.call-update) | async-done | bytes 393232 | tf_op jit(solution)/shard_map/reduce_scatter | solution.py:254
  803.1 236.6 %reduce-scatter.9.cloned.1.call-done = f32[32,5248]{1,0:T(8,128)} async-done(((f32[1024,5248]{1,0:T(8,128)}), f32[32,5248]{1,0:T(8,128)}) %reduce-scatter.9.cloned.1.call-update) | async-done | bytes 671760 | tf_op jit(solution)/shard_map/reduce_scatter | solution.py:256
  (411 shorter events, 140.3 us)
Async XLA Ops:
  7.2 73.5 %all-gather.5.cloned.1.call-start = ((), (), s32[]{:S(2)}) async-start(), calls=%async_computation.4 | async-start | bytes 6488064 | tf_op jit(solution)/shard_map/all_gather | solution.py:120
  7.9 129.8 %all-gather.7.cloned.1.call-start = ((), (), s32[]{:S(2)}) async-start(), calls=%async_computation.5 | async-start | bytes 2162688 | tf_op jit(solution)/shard_map/all_gather | solution.py:121
  8.7 219.0 %all-gather.9.cloned.1.call-start = ((), (), s32[]{:S(2)}) async-start(), calls=%async_computation.6 | async-start | bytes 11083776 | tf_op jit(solution)/shard_map/all_gather | solution.py:122
  9.4 286.3 %all-gather.11.cloned.1.call-start = ((), (), s32[]{:S(2)}) async-start(), calls=%async_computation.7 | async-start | bytes 5677056 | tf_op jit(solution)/shard_map/all_gather | solution.py:123
  10.0 551.3 %reduce-scatter.7.cloned.1.call-start = ((), (), s32[]{:S(2)}) async-start(), calls=%async_computation.9 | async-start | bytes 4325376 | tf_op jit(solution)/shard_map/reduce_scatter | solution.py:255
  13.3 88.7 %copy-start.105 = (f32[256]{0:T(256)}, f32[256]{0:T(256)S(1)}, u32[]{:S(2)}) copy-start(f32[256]{0:T(256)S(1)} %broadcast_multiply_fusion.32) | copy-start | bytes 3076
  13.3 72.2 %copy-start.97 = (f32[256]{0:T(256)}, f32[256]{0:T(256)S(1)}, u32[]{:S(2)}) copy-start(f32[256]{0:T(256)S(1)} %get-tuple-element.151) | copy-start | bytes 3076
  13.3 74.1 %copy-start.95 = (f32[256]{0:T(256)}, f32[256]{0:T(256)S(1)}, u32[]{:S(2)}) copy-start(f32[256]{0:T(256)S(1)} %get-tuple-element.152) | copy-start | bytes 3076
  13.9 71.6 %copy-start.101 = (f32[256]{0:T(256)}, f32[256]{0:T(256)S(1)}, u32[]{:S(2)}) copy-start(f32[256]{0:T(256)S(1)} %add_rsqrt_fusion.1) | copy-start | bytes 3076
  55.6 46.4 %copy-start.70 = (f32[1024]{0:T(1024)}, f32[1024]{0:T(1024)S(1)}, u32[]{:S(2)}) copy-start(f32[1024]{0:T(1024)S(1)} %convert_element_type.185) | copy-start | bytes 12292
  59.3 28.2 %copy-start.99 = (f32[256]{0:T(256)}, f32[256]{0:T(256)S(1)}, u32[]{:S(2)}) copy-start(f32[256]{0:T(256)S(1)} %add_rsqrt_fusion.3) | copy-start | bytes 3076
  60.8 41.3 %copy-start.107 = (f32[256]{0:T(256)}, f32[256]{0:T(256)S(1)}, u32[]{:S(2)}) copy-start(f32[256]{0:T(256)S(1)} %add_rsqrt_fusion.5) | copy-start | bytes 3076
  128.4 13.4 %copy-start.43 = (bf16[16,64,256]{2,1,0:T(8,128)(2,1)}, bf16[16,64,256]{2,1,0:T(8,128)(2,1)S(1)}, u32[]{:S(2)}) copy-start(bf16[16,64,256]{2,1,0:T(8,128)(2,1)S(1)} %convolution_convert_fusion.6) | copy-start | bytes 1572868
  161.5 66.2 %copy-start.8 = (f32[256,1024]{1,0:T(8,128)S(1)}, f32[256,1024]{1,0:T(8,128)}, u32[]{:S(2)}) copy-start(f32[256,1024]{1,0:T(8,128)} %copy-done.7) | copy-start | bytes 3145732
  295.8 15.0 %slice-start = ((s8[10747904]{0:T(1024)(128)(4,1)}), s8[4194304]{0:T(1024)(128)(4,1)S(1)}, s32[]{:S(2)}) async-start(s8[10747904]{0:T(1024)(128)(4,1)} %bitcast.151), calls=%async_computation.12 | async-start | bytes 8388608
  295.8 15.0 %slice-start.1 = ((s8[10747904]{0:T(1024)(128)(4,1)}), s8[4194304]{0:T(1024)(128)(4,1)S(1)}, s32[]{:S(2)}) async-start(s8[10747904]{0:T(1024)(128)(4,1)} %bitcast.151), calls=%async_computation.13 | async-start | bytes 8388608
  326.9 9.5 copy-start.18
  353.2 35.2 %copy-start.16 = (f32[256,1024]{1,0:T(8,128)}, f32[256,1024]{1,0:T(8,128)S(1)}, u32[]{:S(2)}) copy-start(f32[256,1024]{1,0:T(8,128)S(1)} %multiply_add_fusion.2) | copy-start | bytes 3145732
  355.9 285.8 %reduce-scatter.11.cloned.1.call-start = ((), (), s32[]{:S(2)}) async-start(), calls=%async_computation.11 | async-start | bytes 11354112 | tf_op jit(solution)/shard_map/reduce_scatter | solution.py:257
  378.3 424.7 %reduce-scatter.5.cloned.1.call-start = ((), (), s32[]{:S(2)}) async-start(), calls=%async_computation.8 | async-start | bytes 12976128 | tf_op jit(solution)/shard_map/reduce_scatter | solution.py:254
  391.1 12.7 %copy-start.79 = (bf16[256,1024]{0,1:T(8,128)(2,1)}, bf16[256,1024]{0,1:T(8,128)(2,1)S(1)}, u32[]{:S(2)}) copy-start(bf16[256,1024]{0,1:T(8,128)(2,1)S(1)} %copy.109) | copy-start | bytes 1572868
  410.8 11.0 %copy-start.50 = (bf16[256,16,64]{0,2,1:T(8,128)(2,1)}, bf16[256,16,64]{0,2,1:T(8,128)(2,1)S(1)}, u32[]{:S(2)}) copy-start(bf16[256,16,64]{0,2,1:T(8,128)(2,1)S(1)} %get-tuple-element.88) | copy-start | bytes 1572868
  410.8 11.0 %copy-start.51 = (bf16[256,16,64]{0,2,1:T(8,128)(2,1)}, bf16[256,16,64]{0,2,1:T(8,128)(2,1)S(1)}, u32[]{:S(2)}) copy-start(bf16[256,16,64]{0,2,1:T(8,128)(2,1)S(1)} %get-tuple-element.89) | copy-start | bytes 1572868
  412.8 16.4 %copy-start.33 = (bf16[256,16,64]{0,2,1:T(8,128)(2,1)}, bf16[256,16,64]{0,2,1:T(8,128)(2,1)S(1)}, u32[]{:S(2)}) copy-start(bf16[256,16,64]{0,2,1:T(8,128)(2,1)S(1)} %get-tuple-element.93) | copy-start | bytes 1572868
  429.2 13.9 %copy-start.72 = (bf16[16,64,256]{2,1,0:T(8,128)(2,1)}, bf16[16,64,256]{2,1,0:T(8,128)(2,1)S(1)}, u32[]{:S(2)}) copy-start(bf16[16,64,256]{2,1,0:T(8,128)(2,1)S(1)} %convolution_convert_fusion.4) | copy-start | bytes 1572868
  443.1 596.6 %reduce-scatter.9.cloned.1.call-start = ((), (), s32[]{:S(2)}) async-start(), calls=%async_computation.10 | async-start | bytes 22167552 | tf_op jit(solution)/shard_map/reduce_scatter | solution.py:256
  444.3 11.0 %copy-start.14 = (f32[256,1024]{1,0:T(8,128)S(1)}, f32[256,1024]{1,0:T(8,128)}, u32[]{:S(2)}) copy-start(f32[256,1024]{1,0:T(8,128)} %copy-done.11) | copy-start | bytes 3145732
  444.3 11.0 %copy-start.60 = (bf16[256,2624]{1,0:T(8,128)(2,1)S(1)}, bf16[256,2624]{1,0:T(8,128)(2,1)}, u32[]{:S(2)}) copy-start(bf16[256,2624]{1,0:T(8,128)(2,1)} %get-tuple-element.40) | copy-start | bytes 4030468
  444.3 11.0 %copy-start.61 = (bf16[256,2624]{1,0:T(8,128)(2,1)S(1)}, bf16[256,2624]{1,0:T(8,128)(2,1)}, u32[]{:S(2)}) copy-start(bf16[256,2624]{1,0:T(8,128)(2,1)} %get-tuple-element.41) | copy-start | bytes 4030468
  488.2 10.5 %slice-start.5 = ((s8[6291456]{0:T(1024)(128)(4,1)}), s8[4194304]{0:T(1024)(128)(4,1)S(1)}, s32[]{:S(2)}) async-start(s8[6291456]{0:T(1024)(128)(4,1)} %bitcast.212), calls=%async_computation.17 | async-start | bytes 8388608
  543.7 9.8 slice-start.3
  543.7 9.8 slice-start.7
  (101 other events, 375.2 us)
Sparse Core Ops, SparseCore 0:
  10.9 69.7 all-gather.4
  83.5 54.2 all-gather.6
  140.6 87.0 all-gather.8
  230.4 65.2 all-gather.10
  356.1 107.6 reduce-scatter.6
  470.2 171.4 reduce-scatter.10
  648.3 154.6 reduce-scatter.4
  806.0 233.5 reduce-scatter.8
where the time goes:
time: 1050 us
  waiting for transfers between devices  625 us (60%)
  matrix products  249 us (24%)
  blocking collectives  81.2 us (8%)
  local copies, waits for them, and re-layouts  49.3 us (5%)
  other arithmetic  24.8 us (2%)
  between operations  16 us (2%)
    reduce_scatter x1, waiting for transfers between devices, shards(): lax.psum_scatter(summed[2], 'dp', scatter_dimension=0, tiled=True)  237 us
    reduce_scatter x1, waiting for transfers between devices, shards(): lax.psum_scatter(summed[0], 'dp', scatter_dimension=0, tiled=True)  161 us
    unnamed x2, blocking collectives  81.2 us
    reduce_scatter x1, waiting for transfers between devices, shards(): lax.psum_scatter(summed[3], 'dp', scatter_dimension=1, tiled=True)  80.5 us
    all_gather x1, waiting for transfers between devices, weights_now(): lax.all_gather(w_in, 'dp', axis=0, tiled=True)  62.8 us
    all_gather x1, waiting for transfers between devices, weights_now(): lax.all_gather(w_down, 'dp', axis=1, tiled=True)  53.9 us
    dot_general x3, matrix products, shards(): jnp.dot(normed_mlp.T, grad_gate_up, preferred_element_type=jnp.float32)  43.8 us
    dot_general x3, matrix products, shards(): jnp.dot(normed_attn.T, grad_projected, preferred_element_type=jnp.float32)  27 us
  transfers between devices with their start and end apart: 8, of which 7 were waited for; matrix products, arithmetic and copies ran while one was open for 24% of the time, Pallas kernels for 0%

commit v1 on v0

--- a/solution.py
+++ b/solution.py
@@ -10,6 +10,18 @@
 NEG_BIG = -1e30
 ROOT_HALF = 0.7071067811865476
 INV_ROOT_TWO_PI = 0.3989422804014327
+
+
+def collect(x, axis, dim):
+    ways, here, lap = (lax.axis_size(axis), lax.axis_index(axis), x.shape[dim])
+    line, have = (x, 1)
+    while have < ways:
+        line = jnp.concatenate(
+            [line, lax.ppermute(line, axis, [(d, (d - have) % ways) for d in range(ways)])],
+            axis=dim,
+        )
+        have = 2 * have
+    return jnp.roll(line, here * lap, axis=dim)
 
 
 def positions(seg_row):
@@ -119,7 +131,7 @@
         return (
             lax.all_gather(w_qkv, "dp", axis=0, tiled=True),
             lax.all_gather(w_attn_out, "dp", axis=0, tiled=True),
-            lax.all_gather(w_in, "dp", axis=0, tiled=True),
+            collect(w_in, "dp", 0),
             lax.all_gather(w_down, "dp", axis=1, tiled=True),
             lax.all_gather(gain_attn, "dp", axis=0, tiled=True),
             lax.all_gather(gain_mlp, "dp", axis=0, tiled=True),

time: 1050 us -> 1290 us (1.23)
  blocking collectives: 81.2 us -> 295 us
  other arithmetic: 24.8 us -> 40.1 us
  local copies, waits for them, and re-layouts: 49.3 us -> 62.6 us
    unnamed x2, blocking collectives: 81.2 us -> 295 us
    ppermute x0 -> x5, waiting for transfers between devices: none -> 138 us  [collect(): lax.ppermute(line, axis, [(d, (d - have) % ways) for d in range(ways)])]
    all_gather x1 -> x0, waiting for transfers between devices: 62.8 us -> none  [weights_now(): lax.all_gather(w_in, 'dp', axis=0, tiled=True)]
    all_gather x1, waiting for transfers between devices: 53.9 us -> 0.02 us  [weights_now(): lax.all_gather(w_down, 'dp', axis=1, tiled=True)]
    all_gather x1, waiting for transfers between devices: 18.4 us -> 0.02 us  [weights_now(): lax.all_gather(w_qkv, 'dp', axis=0, tiled=True)]
    concatenate x0 -> x4, other arithmetic: none -> 15.8 us  [the longest x1 12.4 us: collect(): return jnp.roll(line, here * lap, axis=dim)]
  transfers between devices with their start and end apart: 8 -> 12, of which waited for: 7 -> 7; matrix products, arithmetic and copies ran while one was open for 24% -> 22% of each run, Pallas kernels for 0% -> 0%
where the time goes in v1:
time: 1290 us
  waiting for transfers between devices  614 us (48%)
  blocking collectives  295 us (23%)
  matrix products  252 us (20%)
  local copies, waits for them, and re-layouts  62.6 us (5%)
  other arithmetic  40.1 us (3%)
  between operations  16.3 us (1%)
    unnamed x2, blocking collectives  295 us
    reduce_scatter x1, waiting for transfers between devices, shards(): lax.psum_scatter(summed[2], 'dp', scatter_dimension=0, tiled=True)  237 us
    reduce_scatter x1, waiting for transfers between devices, shards(): lax.psum_scatter(summed[0], 'dp', scatter_dimension=0, tiled=True)  161 us
    ppermute x5, waiting for transfers between devices, collect(): lax.ppermute(line, axis, [(d, (d - have) % ways) for d in range(ways)])  138 us
    reduce_scatter x1, waiting for transfers between devices, shards(): lax.psum_scatter(summed[3], 'dp', scatter_dimension=1, tiled=True)  77.4 us
    dot_general x3, matrix products, shards(): jnp.dot(normed_mlp.T, grad_gate_up, preferred_element_type=jnp.float32)  45.2 us
    dot_general x3, matrix products, shards(): jnp.dot(grad_gate_up, wi_full.T, preferred_element_type=jnp.float32)  27.3 us
    dot_general x3, matrix products, shards(): jnp.dot(normed_attn.T, grad_projected, preferred_element_type=jnp.float32)  26.8 us
  transfers between devices with their start and end apart: 12, of which 7 were waited for; matrix products, arithmetic and copies ran while one was open for 22% of the time, Pallas kernels for 0%

profile of v1, /device:TPU:14, one launch (start us, length us, event | category | flops | bytes accessed | tf_op | source)
XLA Modules:
  0.0 1287.1 jit_solution(4832170331065162172)
XLA Ops:
  8.0 5.0 collective-permute-done
  15.5 20.0 %collective-permute-done.1 = bf16[64,5248]{1,0:T(8,128)(2,1)S(1)} collective-permute-done((bf16[64,5248]{1,0:T(8,128)(2,1)S(1)}, bf16[64,5248]{1,0:T(8,128)(2,1)S(1)}, u32[]{:S(2)}, u32[]{:S(2)}) %collective-permute-start.1) | collective-permute-done | bytes 671776 | tf_op jit(solution)/shard_map/ppermute | solution.py:20
  37.7 40.4 %collective-permute-done.2 = bf16[128,5248]{1,0:T(8,128)(2,1)S(1)} collective-permute-done((bf16[128,5248]{1,0:T(8,128)(2,1)}, bf16[128,5248]{1,0:T(8,128)(2,1)S(1)}, u32[]{:S(2)}, u32[]{:S(2)}) %collective-permute-start.2) | collective-permute-done | bytes 1343520 | tf_op jit(solution)/shard_map/ppermute | solution.py:20
  83.5 72.7 %collective-permute-done.3 = bf16[256,5248]{1,0:T(8,128)(2,1)S(1)} collective-permute-done((bf16[256,5248]{1,0:T(8,128)(2,1)S(1)}, bf16[256,5248]{1,0:T(8,128)(2,1)S(1)}, u32[]{:S(2)}, u32[]{:S(2)}) %collective-permute-start.3) | collective-permute-done | bytes 2687008 | tf_op jit(solution)/shard_map/ppermute | solution.py:20
  164.1 252.4 %all-reduce.5 = (bf16[1024]{0:T(1024)(128)(2,1)S(1)}, bf16[1024]{0:T(1024)(128)(2,1)S(1)}) all-reduce(bf16[1024]{0:T(1024)(128)(2,1)S(1)} %dynamic-update-slice, bf16[1024]{0:T(1024)(128)(2,1)S(1)} %dynamic-update-slice.1), channel_id=1, replica_groups=mesh['dp'=32] {'dp'}, use_global_device_ids=true, to_apply=%add | all-reduce | flops 2048 | bytes 8192
  424.1 5.3 constant_dynamic-update-slice_fusion.5
  429.4 12.4 fusion.3
  496.5 5.1 fusion.190
  519.3 4.9 fusion.176
  529.1 5.0 fusion.174
  534.1 7.7 fusion.24
  541.9 9.2 fusion.35
  551.1 8.8 fusion.18
  559.9 7.2 multiply_reduce_fusion.4
  567.1 8.4 fusion.12
  575.6 11.0 multiply_add_fusion.1
  597.1 5.7 fusion.114
  602.8 12.0 add_add_fusion.2
  653.4 6.5 fusion.105
  660.8 6.6 fusion.107
  669.0 13.7 %add_add_fusion.1 = f32[1024,3072]{1,0:T(8,128)} fusion(f32[1024,3072]{1,0:T(8,128)} %fusion.105, f32[1024,3072]{1,0:T(8,128)} %fusion.107, bf16[256,1024]{0,1:T(8,128)(2,1)S(1)} %bitcast.187, bf16[256,1024]{0,1:T(8,128)(2,1)S(1)} %bitcast.171, bf16[256,1024]{0,1:T(8,128)(2,1)S(1)} %bitcast.169, f32[1024]{0:T(1024)S(1)} %copy-done.69, ...), kind=kOutput, calls=%fused_computation.6 | convolution fusion | flops 1622933504 | bytes 39852032 | tf_op jit(solution)/shard_map/dot_general | solution.py:254
  682.9 12.7 fusion.34
  695.5 9.4 fusion.36
  705.0 23.1 %add_add_fusion = f32[1024,5248]{1,0:T(8,128)} fusion(f32[1024,5248]{1,0:T(8,128)} %fusion.34, f32[1024,5248]{1,0:T(8,128)} %fusion.36, bf16[256,2624]{1,0:T(8,128)(2,1)S(1)} %copy-done.61, bf16[256,2624]{1,0:T(8,128)(2,1)S(1)} %copy-done.60, f32[256,1024]{1,0:T(8,128)S(1)} %get-tuple-element.149, f32[1024]{0:T(1024)S(1)} %convert_element_type.194, ...), kind=kOutput, calls=%fused_computation.5 | convolution fusion | flops 2768633856 | bytes 68229120 | tf_op jit(solution)/shard_map/dot_general | solution.py:229
  728.2 5.2 fusion.108
  733.5 5.1 fusion.106
  742.4 42.8 %all-reduce.4 = (f32[1024]{0:T(1024)S(1)}, f32[1024]{0:T(1024)S(1)}) all-reduce(f32[1024]{0:T(1024)S(1)} %add_add_fusion.5, f32[1024]{0:T(1024)S(1)} %add_add_fusion.4), channel_id=6, replica_groups=mesh['dp'=32] {'dp'}, use_global_device_ids=true, to_apply=%region_46.48.clone | all-reduce | flops 2048 | bytes 16384
  786.4 5.1 fusion.41
  791.5 5.5 fusion.40
  804.9 77.4 %reduce-scatter.11.cloned.1.call-done = f32[2624,32]{0,1:T(8,128)} async-done(((f32[2624,1024]{0,1:T(8,128)}), f32[2624,32]{0,1:T(8,128)}) %reduce-scatter.11.cloned.1.call-update) | async-done | bytes 335888 | tf_op jit(solution)/shard_map/reduce_scatter | solution.py:269
  882.3 160.8 %reduce-scatter.5.cloned.1.call-done = f32[32,3072]{1,0:T(8,128)} async-done(((f32[1024,3072]{1,0:T(8,128)}), f32[32,3072]{1,0:T(8,128)}) %reduce-scatter.5.cloned.1.call-update) | async-done | bytes 393232 | tf_op jit(solution)/shard_map/reduce_scatter | solution.py:266
  1043.2 236.6 %reduce-scatter.9.cloned.1.call-done = f32[32,5248]{1,0:T(8,128)} async-done(((f32[1024,5248]{1,0:T(8,128)}), f32[32,5248]{1,0:T(8,128)}) %reduce-scatter.9.cloned.1.call-update) | async-done | bytes 671760 | tf_op jit(solution)/shard_map/reduce_scatter | solution.py:268
  (436 shorter events, 166.8 us)
Async XLA Ops:
  7.2 71.0 %copy-start.23 = (bf16[32,5248]{1,0:T(8,128)(2,1)S(1)}, bf16[32,5248]{1,0:T(8,128)(2,1)}, u32[]{:S(2)}) copy-start(bf16[32,5248]{1,0:T(8,128)(2,1)} %param.15) | copy-start | bytes 1007620
  7.2 434.6 %all-gather.4.cloned.1.call-start = ((), (), s32[]{:S(2)}) async-start(), calls=%async_computation.4 | async-start | bytes 6488064 | tf_op jit(solution)/shard_map/all_gather | solution.py:132
  7.9 483.2 %all-gather.6.cloned.1.call-start = ((), (), s32[]{:S(2)}) async-start(), calls=%async_computation.5 | async-start | bytes 2162688 | tf_op jit(solution)/shard_map/all_gather | solution.py:133
  8.0 5.1 collective-permute-start
  14.0 21.5 %collective-permute-start.1 = (bf16[64,5248]{1,0:T(8,128)(2,1)S(1)}, bf16[64,5248]{1,0:T(8,128)(2,1)S(1)}, u32[]{:S(2)}, u32[]{:S(2)}) collective-permute-start(bf16[64,5248]{1,0:T(8,128)(2,1)S(1)} %pad_maximum_fusion.16), channel_id=1, source_target_pairs={{0,30},{1,31},{2,0},{3,1},{4,2},{5,3},{6,4},{7,5},{8,6},{9,7},{10,... | collective-permute-start | bytes 2015240 | tf_op jit(solution)/shard_map/ppermute | solution.py:20
  37.7 40.5 %collective-permute-start.2 = (bf16[128,5248]{1,0:T(8,128)(2,1)}, bf16[128,5248]{1,0:T(8,128)(2,1)S(1)}, u32[]{:S(2)}, u32[]{:S(2)}) collective-permute-start(bf16[128,5248]{1,0:T(8,128)(2,1)} %pad_maximum_fusion.15), channel_id=1, source_target_pairs={{0,28},{1,29},{2,30},{3,31},{4,0},{5,1},{6,2},{7,3},{8,4},{9,5},{1... | collective-permute-start | bytes 4030472 | tf_op jit(solution)/shard_map/ppermute | solution.py:20
  37.7 496.4 %all-gather.8.cloned.1.call-start = ((), (), s32[]{:S(2)}) async-start(), calls=%async_computation.6 | async-start | bytes 5677056 | tf_op jit(solution)/shard_map/all_gather | solution.py:135
  78.4 77.8 %collective-permute-start.3 = (bf16[256,5248]{1,0:T(8,128)(2,1)S(1)}, bf16[256,5248]{1,0:T(8,128)(2,1)S(1)}, u32[]{:S(2)}, u32[]{:S(2)}) collective-permute-start(bf16[256,5248]{1,0:T(8,128)(2,1)S(1)} %pad_maximum_fusion.1), channel_id=1, source_target_pairs={{0,24},{1,25},{2,26},{3,27},{4,28},{5,29},{6,30},{7,31},{8,0},{9,1... | collective-permute-start | bytes 8060936 | tf_op jit(solution)/shard_map/ppermute | solution.py:20
  156.2 260.3 %copy-start.106 = (s32[3,256]{1,0:T(4,128)S(1)}, s32[3,256]{1,0:T(4,128)}, u32[]{:S(2)}) copy-start(s32[3,256]{1,0:T(4,128)} %param.12) | copy-start | bytes 9220
  156.2 264.8 %copy-start.3 = (bf16[768,1024]{1,0:T(8,128)(2,1)S(1)}, bf16[768,1024]{1,0:T(8,128)(2,1)}, u32[]{:S(2)}) copy-start(bf16[768,1024]{1,0:T(8,128)(2,1)} %param.11) | copy-start | bytes 4718596
  158.9 265.2 %collective-permute-start.4 = (bf16[512,5248]{1,0:T(8,128)(2,1)}, bf16[512,5248]{1,0:T(8,128)(2,1)}, u32[]{:S(2)}, u32[]{:S(2)}) collective-permute-start(bf16[512,5248]{1,0:T(8,128)(2,1)} %get-tuple-element.55), channel_id=1, source_target_pairs={{0,16},{1,17},{2,18},{3,19},{4,20},{5,21},{6,22},{7,23},{8,24},{9,... | collective-permute-start | bytes 16121864 | tf_op jit(solution)/shard_map/ppermute | solution.py:20
  163.6 641.3 %reduce-scatter.7.cloned.1.call-start = ((), (), s32[]{:S(2)}) async-start(), calls=%async_computation.8 | async-start | bytes 4325376 | tf_op jit(solution)/shard_map/reduce_scatter | solution.py:267
  416.5 47.3 %copy-start.68 = (f32[1024]{0:T(1024)}, f32[1024]{0:T(1024)S(1)}, u32[]{:S(2)}) copy-start(f32[1024]{0:T(1024)S(1)} %convert_element_type.185) | copy-start | bytes 12292
  421.3 42.5 %copy-start.104 = (f32[256]{0:T(256)}, f32[256]{0:T(256)S(1)}, u32[]{:S(2)}) copy-start(f32[256]{0:T(256)S(1)} %broadcast_multiply_fusion.32) | copy-start | bytes 3076
  421.3 20.5 %copy-start.94 = (f32[256]{0:T(256)}, f32[256]{0:T(256)S(1)}, u32[]{:S(2)}) copy-start(f32[256]{0:T(256)S(1)} %get-tuple-element.162) | copy-start | bytes 3076
  421.3 34.0 %copy-start.92 = (f32[256]{0:T(256)}, f32[256]{0:T(256)S(1)}, u32[]{:S(2)}) copy-start(f32[256]{0:T(256)S(1)} %get-tuple-element.163) | copy-start | bytes 3076
  421.9 19.9 %copy-start.98 = (f32[256]{0:T(256)}, f32[256]{0:T(256)S(1)}, u32[]{:S(2)}) copy-start(f32[256]{0:T(256)S(1)} %add_rsqrt_fusion.1) | copy-start | bytes 3076
  421.9 33.4 %copy-start.96 = (f32[256]{0:T(256)}, f32[256]{0:T(256)S(1)}, u32[]{:S(2)}) copy-start(f32[256]{0:T(256)S(1)} %add_rsqrt_fusion.3) | copy-start | bytes 3076
  421.9 41.9 %copy-start.107 = (f32[256]{0:T(256)}, f32[256]{0:T(256)S(1)}, u32[]{:S(2)}) copy-start(f32[256]{0:T(256)S(1)} %add_rsqrt_fusion.5) | copy-start | bytes 3076
  501.6 132.1 %copy-start.102 = (f32[16,256]{1,0:T(8,128)}, f32[16,256]{1,0:T(8,128)S(1)}, u32[]{:S(2)}) copy-start(f32[16,256]{1,0:T(8,128)S(1)} %get-tuple-element.142) | copy-start | bytes 49156
  508.2 11.0 slice-start
  541.9 18.0 %slice-start.3 = ((s8[10747904]{0:T(1024)(128)(4,1)}), s8[4194304]{0:T(1024)(128)(4,1)S(1)}, s32[]{:S(2)}) async-start(s8[10747904]{0:T(1024)(128)(4,1)} %bitcast.153), calls=%async_computation.14 | async-start | bytes 8388608
  541.9 18.0 %slice-start.4 = ((s8[10747904]{0:T(1024)(128)(4,1)}), s8[4194304]{0:T(1024)(128)(4,1)S(1)}, s32[]{:S(2)}) async-start(s8[10747904]{0:T(1024)(128)(4,1)} %bitcast.153), calls=%async_computation.15 | async-start | bytes 8388608
  575.6 11.0 copy-start.41
  593.9 288.4 %reduce-scatter.11.cloned.1.call-start = ((), (), s32[]{:S(2)}) async-start(), calls=%async_computation.10 | async-start | bytes 11354112 | tf_op jit(solution)/shard_map/reduce_scatter | solution.py:269
  614.9 428.3 %reduce-scatter.5.cloned.1.call-start = ((), (), s32[]{:S(2)}) async-start(), calls=%async_computation.7 | async-start | bytes 12976128 | tf_op jit(solution)/shard_map/reduce_scatter | solution.py:266
  630.1 12.8 copy-start.75
  651.8 16.4 %copy-start.30 = (bf16[256,16,64]{0,2,1:T(8,128)(2,1)}, bf16[256,16,64]{0,2,1:T(8,128)(2,1)S(1)}, u32[]{:S(2)}) copy-start(bf16[256,16,64]{0,2,1:T(8,128)(2,1)S(1)} %get-tuple-element.104) | copy-start | bytes 1572868
  682.8 597.0 %reduce-scatter.9.cloned.1.call-start = ((), (), s32[]{:S(2)}) async-start(), calls=%async_computation.9 | async-start | bytes 22167552 | tf_op jit(solution)/shard_map/reduce_scatter | solution.py:268
  682.8 12.7 copy-start.11
  682.8 12.7 copy-start.58
  682.8 12.7 copy-start.59
  (108 other events, 418.4 us)
Sparse Core Ops, SparseCore 0:
  10.9 109.4 all-gather.3
  123.2 306.0 all-gather.5
  432.2 66.1 all-gather.7
  594.0 110.1 reduce-scatter.6
  710.6 171.6 reduce-scatter.10
  888.8 154.3 reduce-scatter.4
  1046.2 233.6 reduce-scatter.8
